TPU v7x, 32 devices: a whole 2x2x4 slice. The times are simulated.
32 devices in a mesh: grp: 4 (over x, core), row: 8 (over z, y).
Axes of the slice: x: 2, y: 2, z: 4, core: 2. Of those that a mesh axis runs over, the one named last changes fastest.
Arguments:
- features: bfloat16 [2048, 4096], P('row', 'grp'), may hold values from -0.125 to 0.125
- residual: float32 [2048, 576], P('row'), may hold values from -6 to 6
- precond: float32 [4096, 1024], P('grp'), as said below
Outputs:
- coefs: float32 [4096, 576], P('grp')
- section_resid: float32 [4, 2048, 576], P('grp', 'row')
Inputs may be any that keep to these rules, and one draw needn't show every extreme that they name: Each 1024 x 1024 block of precond is symmetric and positive definite.
All inputs are finite; a program needn't handle non-finite values.
Results may differ from a plain program's by a relative error of at most 0.009.
Values may be sent and summed in bfloat16 or wider, within the bound.
No kernel may reach another device: no remote copies, remote signals or barrier semaphores. Data moves between devices by JAX's collectives and lax.ppermute only.
A program may use at most 64 MiB of HBM per device.

v0:
```python
import jax
import jax.numpy as jnp
from jax import lax
from jax.sharding import PartitionSpec as P


def from_behind(block, axis, distance):
    devices = range(lax.axis_size(axis))
    route = [(i - distance, i) for i in devices if i - distance in devices]
    return lax.ppermute(block, axis, route)


def chain_sweep(features, residual, precond):
    section_index = lax.axis_index("grp")
    section_count = lax.axis_size("grp")
    row_count, target_width = residual.shape
    block_width = features.shape[1]
    panel_count = 3
    panel_width = target_width // panel_count
    step_count = section_count + panel_count - 1

    def correlate(rounded):
        correlation = lax.dot_general(
            features, rounded, (((0,), (0,)), ((), ())), preferred_element_type=jnp.float32
        )
        correlation = lax.psum(correlation, "row")
        return jnp.dot(precond, correlation, precision=lax.Precision.HIGHEST)

    def turn(turn_index, loop_state):
        current, coef_table, resid_table = loop_state
        position = turn_index - section_index
        inside = jnp.logical_and(position >= 0, position < panel_count)
        panel_slot = jnp.clip(position, 0, panel_count - 1) * panel_width
        fresh_panel = lax.dynamic_slice_in_dim(residual, panel_slot, panel_width, 1)
        current = jnp.where(section_index == 0, fresh_panel, current)
        rounded = current.astype(jnp.bfloat16)
        coefficient = correlate(rounded)
        updated = current - jnp.dot(
            features, coefficient.astype(jnp.bfloat16), preferred_element_type=jnp.float32
        )
        old_coef = lax.dynamic_slice_in_dim(coef_table, panel_slot, panel_width, 1)
        coef_table = lax.dynamic_update_slice_in_dim(
            coef_table, jnp.where(inside, coefficient, old_coef), panel_slot, 1
        )
        old_resid = lax.dynamic_slice_in_dim(resid_table, panel_slot, panel_width, 2)
        resid_table = lax.dynamic_update_slice_in_dim(
            resid_table, jnp.where(inside, updated[None], old_resid), panel_slot, 2
        )
        passed = from_behind(updated, "grp", 1)
        return (passed, coef_table, resid_table)

    start_state = (
        jnp.zeros((row_count, panel_width), jnp.float32),
        jnp.zeros((block_width, target_width), jnp.float32),
        jnp.zeros((1, row_count, target_width), jnp.float32),
    )
    final_state = lax.fori_loop(0, step_count, turn, start_state)
    return (final_state[1], final_state[2])


def local(features, residual, precond):
    return chain_sweep(features, residual, precond)


def solution(mesh):
    placed = (P("row", "grp"), P("row", None), P("grp", None))
    return jax.shard_map(
        local,
        mesh=mesh,
        in_specs=placed,
        out_specs=(P("grp", None), P("grp", "row", None)),
        check_vma=False,
    )
```

profile of v0, /device:TPU:1, one launch (start us, length us, event | category | flops | bytes accessed | tf_op | source)
XLA Modules:
  0.0 584.3 jit_solution(12787085232364067102)
XLA Ops:
  7.2 0.9 broadcast_in_dim.19
  8.1 0.3 broadcast_in_dim.18
  8.3 567.7 %while.18 = (s32[]{:T(128)}, f32[256,192]{0,1:T(8,128)S(1)}, f32[1024,576]{0,1:T(8,128)S(1)}, f32[1,256,576]{1,2,0:T(8,128)}, pred[]{:T(512)}, /*index=5*/s32[]{...) while((s32[]{:T(128)}, f32[256,192]{0,1:T(8,128)S(1)}, ...), condition=%wide.region_2.3_spmd, body=%wide.region_0.2_spmd.sunk | while | flops 2618032128 | bytes 20677516 | solution.py:57
  8.4 0.0 all-reduce.2.cloned.1.call-start
  8.4 2.1 convolution_bitcast_fusion.4
  10.5 0.0 all-reduce.2.cloned.1.call-update
  10.5 78.6 %all-reduce.2.cloned.1.call-done = f32[1024,192]{0,1:T(8,128)} async-done(((f32[1024,192]{0,1:T(8,128)}), f32[1024,192]{0,1:T(8,128)}) %all-reduce.2.cloned.1.call-update) | async-done | bytes 786448 | tf_op jit(solution)/shard_map/while/body/eval_jaxpr/psum | solution.py:26
  89.2 6.3 %select_dynamic-update-slice_fusion.2 = (f32[1024,576]{0,1:T(8,128)S(1)}, bf16[1024,192]{0,1:T(8,128)(2,1)S(1)}) fusion(f32[1024,576]{0,1:T(8,128)S(1)} %get-tuple-element.285, s32[]{:T(128)S(6)} %select_n.97, pred[]{:T(512)S(6)} %and.10, f32[1024,192]{0,1:T(8,128)} %all-reduce.2.cloned.1.call-done, f32[1024,1024]{1,0:T(8,128)} %get-tuple-element.306), kind=kOutput, calls=%fused_computation.4.clone.1 | convolution fusion | flops 2416312320 | bytes 6946821 | tf_op jit(solution)/shard_map/while/body/eval_jaxpr/dot_general | solution.py:27
  95.5 1.3 fusion.23
  96.8 0.8 copy-done.3
  97.6 4.8 collective-permute-start
  102.4 2.6 collective-permute-done
  105.0 2.1 convolution_bitcast_fusion.4
  107.1 76.5 %all-reduce.2.cloned.1.call-done = f32[1024,192]{0,1:T(8,128)} async-done(((f32[1024,192]{0,1:T(8,128)}), f32[1024,192]{0,1:T(8,128)}) %all-reduce.2.cloned.1.call-update) | async-done | bytes 786448 | tf_op jit(solution)/shard_map/while/body/eval_jaxpr/psum | solution.py:26
  183.6 6.3 %select_dynamic-update-slice_fusion.2 = (f32[1024,576]{0,1:T(8,128)S(1)}, bf16[1024,192]{0,1:T(8,128)(2,1)S(1)}) fusion(f32[1024,576]{0,1:T(8,128)S(1)} %get-tuple-element.285, s32[]{:T(128)S(6)} %select_n.97, pred[]{:T(512)S(6)} %and.10, f32[1024,192]{0,1:T(8,128)} %all-reduce.2.cloned.1.call-done, f32[1024,1024]{1,0:T(8,128)} %get-tuple-element.306), kind=kOutput, calls=%fused_computation.4.clone.1 | convolution fusion | flops 2416312320 | bytes 6946821 | tf_op jit(solution)/shard_map/while/body/eval_jaxpr/dot_general | solution.py:27
  189.9 1.3 fusion.23
  191.2 0.8 copy-done.3
  192.0 4.8 collective-permute-start
  196.8 2.6 collective-permute-done
  199.4 2.1 convolution_bitcast_fusion.4
  201.5 76.5 %all-reduce.2.cloned.1.call-done = f32[1024,192]{0,1:T(8,128)} async-done(((f32[1024,192]{0,1:T(8,128)}), f32[1024,192]{0,1:T(8,128)}) %all-reduce.2.cloned.1.call-update) | async-done | bytes 786448 | tf_op jit(solution)/shard_map/while/body/eval_jaxpr/psum | solution.py:26
  278.0 6.3 %select_dynamic-update-slice_fusion.2 = (f32[1024,576]{0,1:T(8,128)S(1)}, bf16[1024,192]{0,1:T(8,128)(2,1)S(1)}) fusion(f32[1024,576]{0,1:T(8,128)S(1)} %get-tuple-element.285, s32[]{:T(128)S(6)} %select_n.97, pred[]{:T(512)S(6)} %and.10, f32[1024,192]{0,1:T(8,128)} %all-reduce.2.cloned.1.call-done, f32[1024,1024]{1,0:T(8,128)} %get-tuple-element.306), kind=kOutput, calls=%fused_computation.4.clone.1 | convolution fusion | flops 2416312320 | bytes 6946821 | tf_op jit(solution)/shard_map/while/body/eval_jaxpr/dot_general | solution.py:27
  284.4 1.3 fusion.23
  285.6 0.8 copy-done.3
  286.4 4.8 collective-permute-start
  291.3 2.6 collective-permute-done
  293.9 2.1 convolution_bitcast_fusion.4
  296.0 76.1 %all-reduce.2.cloned.1.call-done = f32[1024,192]{0,1:T(8,128)} async-done(((f32[1024,192]{0,1:T(8,128)}), f32[1024,192]{0,1:T(8,128)}) %all-reduce.2.cloned.1.call-update) | async-done | bytes 786448 | tf_op jit(solution)/shard_map/while/body/eval_jaxpr/psum | solution.py:26
  372.1 6.3 %select_dynamic-update-slice_fusion.2 = (f32[1024,576]{0,1:T(8,128)S(1)}, bf16[1024,192]{0,1:T(8,128)(2,1)S(1)}) fusion(f32[1024,576]{0,1:T(8,128)S(1)} %get-tuple-element.285, s32[]{:T(128)S(6)} %select_n.97, pred[]{:T(512)S(6)} %and.10, f32[1024,192]{0,1:T(8,128)} %all-reduce.2.cloned.1.call-done, f32[1024,1024]{1,0:T(8,128)} %get-tuple-element.306), kind=kOutput, calls=%fused_computation.4.clone.1 | convolution fusion | flops 2416312320 | bytes 6946821 | tf_op jit(solution)/shard_map/while/body/eval_jaxpr/dot_general | solution.py:27
  378.4 1.3 fusion.23
  379.7 0.8 copy-done.3
  380.5 4.8 collective-permute-start
  385.4 2.6 collective-permute-done
  387.9 2.1 convolution_bitcast_fusion.4
  390.1 76.1 %all-reduce.2.cloned.1.call-done = f32[1024,192]{0,1:T(8,128)} async-done(((f32[1024,192]{0,1:T(8,128)}), f32[1024,192]{0,1:T(8,128)}) %all-reduce.2.cloned.1.call-update) | async-done | bytes 786448 | tf_op jit(solution)/shard_map/while/body/eval_jaxpr/psum | solution.py:26
  466.1 6.3 %select_dynamic-update-slice_fusion.2 = (f32[1024,576]{0,1:T(8,128)S(1)}, bf16[1024,192]{0,1:T(8,128)(2,1)S(1)}) fusion(f32[1024,576]{0,1:T(8,128)S(1)} %get-tuple-element.285, s32[]{:T(128)S(6)} %select_n.97, pred[]{:T(512)S(6)} %and.10, f32[1024,192]{0,1:T(8,128)} %all-reduce.2.cloned.1.call-done, f32[1024,1024]{1,0:T(8,128)} %get-tuple-element.306), kind=kOutput, calls=%fused_computation.4.clone.1 | convolution fusion | flops 2416312320 | bytes 6946821 | tf_op jit(solution)/shard_map/while/body/eval_jaxpr/dot_general | solution.py:27
  472.4 1.3 fusion.23
  473.7 0.8 copy-done.3
  474.5 4.8 collective-permute-start
  479.4 2.6 collective-permute-done
  482.0 2.1 convolution_bitcast_fusion.4
  484.1 76.1 %all-reduce.2.cloned.1.call-done = f32[1024,192]{0,1:T(8,128)} async-done(((f32[1024,192]{0,1:T(8,128)}), f32[1024,192]{0,1:T(8,128)}) %all-reduce.2.cloned.1.call-update) | async-done | bytes 786448 | tf_op jit(solution)/shard_map/while/body/eval_jaxpr/psum | solution.py:26
  560.2 6.3 %select_dynamic-update-slice_fusion.2 = (f32[1024,576]{0,1:T(8,128)S(1)}, bf16[1024,192]{0,1:T(8,128)(2,1)S(1)}) fusion(f32[1024,576]{0,1:T(8,128)S(1)} %get-tuple-element.285, s32[]{:T(128)S(6)} %select_n.97, pred[]{:T(512)S(6)} %and.10, f32[1024,192]{0,1:T(8,128)} %all-reduce.2.cloned.1.call-done, f32[1024,1024]{1,0:T(8,128)} %get-tuple-element.306), kind=kOutput, calls=%fused_computation.4.clone.1 | convolution fusion | flops 2416312320 | bytes 6946821 | tf_op jit(solution)/shard_map/while/body/eval_jaxpr/dot_general | solution.py:27
  566.5 1.3 fusion.23
  567.8 0.8 copy-done.3
  568.6 4.8 collective-permute-start
  573.4 2.6 collective-permute-done
  576.0 1.4 copy-done.1
  (32 shorter events, 0.2 us)
Async XLA Ops:
  7.2 1.2 copy-start
  8.4 80.8 %all-reduce.2.cloned.1.call-start = ((), (), s32[]{:S(2)}) async-start(), calls=%async_computation | async-start | bytes 1572864 | tf_op jit(solution)/shard_map/while/body/eval_jaxpr/psum | solution.py:26
  89.2 6.3 %copy-start.2 = (f32[1,256,576]{1,2,0:T(8,128)S(1)}, f32[1,256,576]{1,2,0:T(8,128)}, u32[]{:S(2)}) copy-start(f32[1,256,576]{1,2,0:T(8,128)} %get-tuple-element.286) | copy-start | bytes 1769476 | tf_op jit(solution)/shard_map/while
  96.7 0.8 copy-start.3
  97.6 7.4 %collective-permute-start = (f32[256,192]{0,1:T(8,128)S(1)}, f32[256,192]{0,1:T(8,128)S(1)}, u32[]{:S(2)}, u32[]{:S(2)}) collective-permute-start(f32[256,192]{0,1:T(8,128)S(1)} %get-tuple-element.265), channel_id=1, source_target_pairs={{0,8},{8,16},{16,24},{1,9},{9,17},{17,25},{2,10},{10,18},{18,26},{... | collective-permute-start | bytes 589832 | tf_op jit(solution)/shard_map/while/body/eval_jaxpr/ppermute | solution.py:10
  105.0 78.6 %all-reduce.2.cloned.1.call-start = ((), (), s32[]{:S(2)}) async-start(), calls=%async_computation | async-start | bytes 1572864 | tf_op jit(solution)/shard_map/while/body/eval_jaxpr/psum | solution.py:26
  183.6 6.3 %copy-start.2 = (f32[1,256,576]{1,2,0:T(8,128)S(1)}, f32[1,256,576]{1,2,0:T(8,128)}, u32[]{:S(2)}) copy-start(f32[1,256,576]{1,2,0:T(8,128)} %get-tuple-element.286) | copy-start | bytes 1769476 | tf_op jit(solution)/shard_map/while
  191.2 0.8 copy-start.3
  192.0 7.4 %collective-permute-start = (f32[256,192]{0,1:T(8,128)S(1)}, f32[256,192]{0,1:T(8,128)S(1)}, u32[]{:S(2)}, u32[]{:S(2)}) collective-permute-start(f32[256,192]{0,1:T(8,128)S(1)} %get-tuple-element.265), channel_id=1, source_target_pairs={{0,8},{8,16},{16,24},{1,9},{9,17},{17,25},{2,10},{10,18},{18,26},{... | collective-permute-start | bytes 589832 | tf_op jit(solution)/shard_map/while/body/eval_jaxpr/ppermute | solution.py:10
  199.4 78.6 %all-reduce.2.cloned.1.call-start = ((), (), s32[]{:S(2)}) async-start(), calls=%async_computation | async-start | bytes 1572864 | tf_op jit(solution)/shard_map/while/body/eval_jaxpr/psum | solution.py:26
  278.0 6.3 %copy-start.2 = (f32[1,256,576]{1,2,0:T(8,128)S(1)}, f32[1,256,576]{1,2,0:T(8,128)}, u32[]{:S(2)}) copy-start(f32[1,256,576]{1,2,0:T(8,128)} %get-tuple-element.286) | copy-start | bytes 1769476 | tf_op jit(solution)/shard_map/while
  285.6 0.8 copy-start.3
  286.4 7.4 %collective-permute-start = (f32[256,192]{0,1:T(8,128)S(1)}, f32[256,192]{0,1:T(8,128)S(1)}, u32[]{:S(2)}, u32[]{:S(2)}) collective-permute-start(f32[256,192]{0,1:T(8,128)S(1)} %get-tuple-element.265), channel_id=1, source_target_pairs={{0,8},{8,16},{16,24},{1,9},{9,17},{17,25},{2,10},{10,18},{18,26},{... | collective-permute-start | bytes 589832 | tf_op jit(solution)/shard_map/while/body/eval_jaxpr/ppermute | solution.py:10
  293.9 78.2 %all-reduce.2.cloned.1.call-start = ((), (), s32[]{:S(2)}) async-start(), calls=%async_computation | async-start | bytes 1572864 | tf_op jit(solution)/shard_map/while/body/eval_jaxpr/psum | solution.py:26
  372.1 6.3 %copy-start.2 = (f32[1,256,576]{1,2,0:T(8,128)S(1)}, f32[1,256,576]{1,2,0:T(8,128)}, u32[]{:S(2)}) copy-start(f32[1,256,576]{1,2,0:T(8,128)} %get-tuple-element.286) | copy-start | bytes 1769476 | tf_op jit(solution)/shard_map/while
  379.7 0.8 copy-start.3
  380.5 7.4 %collective-permute-start = (f32[256,192]{0,1:T(8,128)S(1)}, f32[256,192]{0,1:T(8,128)S(1)}, u32[]{:S(2)}, u32[]{:S(2)}) collective-permute-start(f32[256,192]{0,1:T(8,128)S(1)} %get-tuple-element.265), channel_id=1, source_target_pairs={{0,8},{8,16},{16,24},{1,9},{9,17},{17,25},{2,10},{10,18},{18,26},{... | collective-permute-start | bytes 589832 | tf_op jit(solution)/shard_map/while/body/eval_jaxpr/ppermute | solution.py:10
  387.9 78.2 %all-reduce.2.cloned.1.call-start = ((), (), s32[]{:S(2)}) async-start(), calls=%async_computation | async-start | bytes 1572864 | tf_op jit(solution)/shard_map/while/body/eval_jaxpr/psum | solution.py:26
  466.1 6.3 %copy-start.2 = (f32[1,256,576]{1,2,0:T(8,128)S(1)}, f32[1,256,576]{1,2,0:T(8,128)}, u32[]{:S(2)}) copy-start(f32[1,256,576]{1,2,0:T(8,128)} %get-tuple-element.286) | copy-start | bytes 1769476 | tf_op jit(solution)/shard_map/while
  473.7 0.8 copy-start.3
  474.5 7.4 %collective-permute-start = (f32[256,192]{0,1:T(8,128)S(1)}, f32[256,192]{0,1:T(8,128)S(1)}, u32[]{:S(2)}, u32[]{:S(2)}) collective-permute-start(f32[256,192]{0,1:T(8,128)S(1)} %get-tuple-element.265), channel_id=1, source_target_pairs={{0,8},{8,16},{16,24},{1,9},{9,17},{17,25},{2,10},{10,18},{18,26},{... | collective-permute-start | bytes 589832 | tf_op jit(solution)/shard_map/while/body/eval_jaxpr/ppermute | solution.py:10
  482.0 78.2 %all-reduce.2.cloned.1.call-start = ((), (), s32[]{:S(2)}) async-start(), calls=%async_computation | async-start | bytes 1572864 | tf_op jit(solution)/shard_map/while/body/eval_jaxpr/psum | solution.py:26
  560.2 6.3 %copy-start.2 = (f32[1,256,576]{1,2,0:T(8,128)S(1)}, f32[1,256,576]{1,2,0:T(8,128)}, u32[]{:S(2)}) copy-start(f32[1,256,576]{1,2,0:T(8,128)} %get-tuple-element.286) | copy-start | bytes 1769476 | tf_op jit(solution)/shard_map/while
  567.8 0.8 copy-start.3
  568.6 7.4 %collective-permute-start = (f32[256,192]{0,1:T(8,128)S(1)}, f32[256,192]{0,1:T(8,128)S(1)}, u32[]{:S(2)}, u32[]{:S(2)}) collective-permute-start(f32[256,192]{0,1:T(8,128)S(1)} %get-tuple-element.265), channel_id=1, source_target_pairs={{0,8},{8,16},{16,24},{1,9},{9,17},{17,25},{2,10},{10,18},{18,26},{... | collective-permute-start | bytes 589832 | tf_op jit(solution)/shard_map/while/body/eval_jaxpr/ppermute | solution.py:10
  576.0 1.4 copy-start.1
Sparse Core Ops, SparseCore 0:
  13.2 75.9 all-reduce.1
  109.8 73.7 all-reduce.1
  204.2 73.7 all-reduce.1
  298.3 73.7 all-reduce.1
  392.4 73.6 all-reduce.1
  486.4 73.6 all-reduce.1
where the time goes:
time: 585 us; the launch traced here: 584 us
  waiting for transfers between devices  475 us (81%)
  matrix products  57.9 us (10%)
  starting transfers between devices  29 us (5%)
  between operations  14 us (2%)
  local copies, waits for them, and re-layouts  7.44 us (1%)
    psum x6, waiting for transfers between devices, correlate(): correlation = lax.psum(correlation, 'row')  460 us
    dot_general x6, matrix products, correlate(): return jnp.dot(precond, correlation, precision=lax.Precision.HIGHEST)  37.8 us
    ppermute x6, starting transfers between devices, from_behind(): return lax.ppermute(block, axis, route)  29 us
    ppermute x6, waiting for transfers between devices, from_behind(): return lax.ppermute(block, axis, route)  15.5 us
    dot_general x6, matrix products, correlate(): lax.dot_general(features, rounded, (((0,), (0,)), ((), ())), preferred_el...  12.5 us
  transfers between devices with their start and end apart: 12, of which 12 were waited for; matrix products, arithmetic and copies ran while one was open for 0% of the time, Pallas kernels for 0%

commit v1 on v0

v1 whole, which is shorter than its diff:
```python
import functools

import jax
import jax.numpy as jnp
from jax import lax
from jax.experimental import pallas as pl
from jax.experimental.pallas import tpu as pltpu
from jax.sharding import PartitionSpec as P

F32 = jnp.float32
BF16 = jnp.bfloat16
CORES = 2
PAIR = 2
ANY = pl.BlockSpec(memory_space=pl.ANY)
VMEM = pl.BlockSpec(memory_space=pltpu.VMEM)
SMEM = pl.BlockSpec(memory_space=pltpu.SMEM)


def pick_copy(use_own, own, other, dst, sem):
    @pl.when(use_own)
    def _():
        pltpu.make_async_copy(own, dst, sem).start()

    @pl.when(jnp.logical_not(use_own))
    def _():
        pltpu.make_async_copy(other, dst, sem).start()

    return pltpu.make_async_copy(own, dst, sem).wait


def correlate_into(r_ref, rows, waits, blocks, c_ref):
    total = None
    for q, wait in enumerate(waits):
        wait()
        part = jnp.dot(
            r_ref[:, q * rows:(q + 1) * rows].astype(BF16),
            blocks[q],
            preferred_element_type=F32,
        )
        total = part if total is None else total + part
    c_ref[...] = total.astype(BF16)


def first_kernel(count, mine_ref, r_ref, *refs):
    own, other = refs[:count], refs[count:2 * count]
    c_ref, blocks, sems = refs[2 * count:]
    use_own = mine_ref[0] == 1
    waits = [pick_copy(use_own, own[q], other[q], blocks.at[q], sems.at[q]) for q in range(count)]
    correlate_into(r_ref, own[0].shape[0], waits, blocks, c_ref)


def stage_kernel(count, has_next, mine_ref, r_ref, ca_ref, cb_ref, *refs):
    own, other = refs[:count], refs[count:2 * count]
    maps = refs[2 * count:2 * count + 4]
    outs = refs[2 * count + 4:]
    if has_next:
        w_ref, rn_ref, rb_ref, cn_ref, blocks, upper, lower, nexts, sems, map_sems, next_sems = outs
    else:
        w_ref, rn_ref, rb_ref, blocks, upper, lower, sems, map_sems = outs
    use_own = mine_ref[0] == 1
    map_waits = [
        pick_copy(use_own, maps[0], maps[1], upper, map_sems.at[0]),
        pick_copy(use_own, maps[2], maps[3], lower, map_sems.at[1]),
    ]
    waits = [pick_copy(use_own, own[q], other[q], blocks.at[q], sems.at[q]) for q in range(count)]
    if has_next:
        next_waits = [
            pick_copy(use_own, other[q], own[q], nexts.at[q], next_sems.at[q]) for q in range(count)
        ]
    rows = own[0].shape[0]
    total = ca_ref[...].astype(F32) + cb_ref[...].astype(F32)
    high = total.astype(BF16)
    low = (total - high.astype(F32)).astype(BF16)
    map_waits[0]()
    w = jnp.dot(high, upper[...], preferred_element_type=F32)
    w += jnp.dot(low, upper[...], preferred_element_type=F32)
    map_waits[1]()
    w += jnp.dot(high, lower[...], preferred_element_type=F32)
    wb = w.astype(BF16)
    w_ref[...] = wb
    for q in range(count):
        waits[q]()
        span = pl.ds(q * rows, rows)
        fresh = r_ref[:, span] - lax.dot_general(
            wb, blocks[q], (((1,), (1,)), ((), ())), preferred_element_type=F32
        )
        rn_ref[:, span] = fresh
        rb_ref[:, span] = fresh.astype(BF16)
    if has_next:
        correlate_into(rn_ref, rows, next_waits, nexts, cn_ref)


def first_call(mine, panel, own, other):
    count = len(own)
    rows, feats = own[0].shape
    width = panel.shape[0]
    return pl.pallas_call(
        functools.partial(first_kernel, count),
        out_shape=jax.ShapeDtypeStruct((width, feats), BF16),
        in_specs=[SMEM, VMEM] + [ANY] * (2 * count),
        out_specs=VMEM,
        scratch_shapes=[pltpu.VMEM((count, rows, feats), BF16), pltpu.SemaphoreType.DMA((count,))],
        cost_estimate=pl.CostEstimate(
            flops=2 * width * rows * count * feats, bytes_accessed=2 * rows * count * feats, transcendentals=0
        ),
        name="first_corr",
    )(mine, panel, *own, *other)


def stage_call(mine, panel, ca, cb, own, other, maps, has_next):
    count = len(own)
    rows, feats = own[0].shape
    width = panel.shape[0]
    wide = jax.ShapeDtypeStruct((width, feats), BF16)
    out_shape = [
        wide,
        jax.ShapeDtypeStruct(panel.shape, F32),
        jax.ShapeDtypeStruct(panel.shape, BF16),
    ]
    scratch = [
        pltpu.VMEM((count, rows, feats), BF16),
        pltpu.VMEM((feats, feats), BF16),
        pltpu.VMEM((feats, feats), BF16),
    ]
    sems = [pltpu.SemaphoreType.DMA((count,)), pltpu.SemaphoreType.DMA((2,))]
    if has_next:
        out_shape.append(wide)
        scratch.append(pltpu.VMEM((count, rows, feats), BF16))
        sems.append(pltpu.SemaphoreType.DMA((count,)))
    return pl.pallas_call(
        functools.partial(stage_kernel, count, has_next),
        out_shape=out_shape,
        in_specs=[SMEM] + [VMEM] * 3 + [ANY] * (2 * count + 4),
        out_specs=[VMEM] * len(out_shape),
        scratch_shapes=scratch + sems,
        cost_estimate=pl.CostEstimate(
            flops=2 * width * feats * (3 * feats + (1 + has_next) * rows * count),
            bytes_accessed=2 * feats * (2 * feats + (1 + has_next) * rows * count),
            transcendentals=0,
        ),
        name="sweep_stage",
    )(mine, panel, ca, cb, *own, *other, *maps)


def sweep(features, residual, precond):
    grp_count, row_count = lax.axis_size("grp"), lax.axis_size("row")
    g, r = lax.axis_index("grp"), lax.axis_index("row")
    core = g % CORES
    plane = g // CORES
    plane_count = grp_count // CORES
    rows, feats = features.shape
    targets = residual.shape[1]
    panel_count = row_count // PAIR * CORES
    width = targets // panel_count

    def permute(x, mask=0, flip=0, keep=None, shift=0):
        route = []
        for a in range(grp_count):
            if keep is not None and a % CORES != keep:
                continue
            b = (a ^ flip) + shift
            if b >= grp_count:
                continue
            for i in range(row_count):
                route.append((a * row_count + i, b * row_count + (i ^ mask)))
        return lax.ppermute(x, ("grp", "row"), route)

    bits = [1 << i for i in range(row_count.bit_length() - 1) if (1 << i) != PAIR]
    masks = [0]
    for bit in reversed(bits):
        masks += [m ^ bit for m in masks]

    def place_of(index):
        return (index // (2 * PAIR)) * PAIR + index % PAIR

    own = {0: features}
    for bit in reversed(bits):
        for m in list(own):
            own[m ^ bit] = permute(own[m], mask=bit)
    own = [own[m] for m in masks]
    upper = precond.astype(BF16)
    lower = (precond - upper.astype(F32)).astype(BF16)
    upper_other = permute(upper, flip=1)
    lower_other = permute(lower, flip=1)
    maps = (upper, upper_other, lower, lower_other)
    other = [permute(a, flip=1) for a in own]

    turned = residual.T

    def slice_for(mask):
        at = (place_of(r ^ mask) * CORES + core) * width
        return lax.dynamic_slice_in_dim(turned, at, width, 0)

    panel = jnp.concatenate(
        [slice_for(0)] + [permute(slice_for(m), mask=m) for m in masks[1:]], axis=1
    )

    first_mine = jnp.where(core == 0, 1, 0).astype(jnp.int32).reshape(1)
    second_mine = 1 - first_mine
    maps_swap = maps

    keep_first = keep_second = base = None
    passed = None
    for step in range(plane_count):
        here = plane == step
        corr = first_call(first_mine, panel, own, other)
        w1, panel1, _, corr = stage_call(
            first_mine, panel, corr, permute(corr, mask=PAIR), own, other, maps, True
        )[0:4]
        w2, _, panel2 = stage_call(
            second_mine, panel1, corr, permute(corr, mask=PAIR), own, other, maps_swap, False
        )
        keep_first = w1 if keep_first is None else jnp.where(here, w1, keep_first)
        keep_second = w2 if keep_second is None else jnp.where(here, w2, keep_second)
        if step + 1 < plane_count:
            moved = permute(panel2, shift=CORES)
            passed = moved if passed is None else jnp.where(plane == step + 1, moved, passed)
            panel = moved.astype(F32)

    def gather(kept, which):
        sent = permute(kept, flip=1, keep=1 - which)
        pair = jnp.concatenate((kept, sent) if which == 0 else (sent, kept), axis=0)
        held = {0: pair}
        for bit in reversed(bits):
            for m in list(held):
                held[m ^ bit] = permute(held[m], mask=bit, keep=which)
        return [held[m] for m in masks]

    first_parts = gather(keep_first, 0)
    second_parts = gather(keep_second, 1)
    coef_t = jnp.zeros((targets, feats), BF16)
    for m, a, b in zip(masks, first_parts, second_parts):
        part = jnp.where(core == 0, a, b)
        coef_t = lax.dynamic_update_slice_in_dim(coef_t, part, place_of(r ^ m) * CORES * width, 0)

    base_t = turned
    if passed is not None:
        sibling = permute(passed, flip=1)
        pair = jnp.where(
            core == 0,
            jnp.concatenate((passed, sibling), axis=0),
            jnp.concatenate((sibling, passed), axis=0),
        )
        for k, m in enumerate(masks):
            block = pair[:, k * rows:(k + 1) * rows]
            block = permute(block, mask=m) if m else block
            start = place_of(r ^ m) * CORES * width
            old = lax.dynamic_slice_in_dim(turned, start, CORES * width, 0)
            base_t = lax.dynamic_update_slice_in_dim(
                base_t, jnp.where(plane == 0, old, block.astype(F32)), start, 0
            )
    change_t = lax.dot_general(
        coef_t, features, (((1,), (1,)), ((), ())), preferred_element_type=F32
    )
    after_t = base_t - change_t
    before_t = permute(after_t, flip=1, keep=0)
    resid_t = jnp.where(core == 0, after_t, before_t - change_t)
    return coef_t.T.astype(F32), resid_t.T[None]


def solution(mesh):
    placed = (P("row", "grp"), P("row", None), P("grp", None))
    return jax.shard_map(
        sweep,
        mesh=mesh,
        in_specs=placed,
        out_specs=(P("grp", None), P("grp", "row", None)),
        check_vma=False,
    )
```

time: 585 us -> 181 us (0.31)
  waiting for transfers between devices: 475 us -> 70.8 us
  matrix products: 57.9 us -> 1.58 us
  Pallas kernels: 0 us -> 36.4 us
  starting transfers between devices: 29 us -> 53.9 us
  between operations: 14 us -> 1.07 us
  other arithmetic: 0 us -> 10.8 us
    psum x6 -> x0, waiting for transfers between devices: 460 us -> none  [correlate(): correlation = lax.psum(correlation, 'row')]
    dot_general x18 -> x1, matrix products: 57.9 us -> 1.58 us  [sweep(): lax.dot_general(coef_t, features, (((1,), (1,)), ((), ())), preferred_ele...]
    ppermute x6 -> x30, waiting for transfers between devices: 15.5 us -> 70.8 us  [permute(): return lax.ppermute(x, ('grp', 'row'), route)]
    pallas_call x0 -> x6, Pallas kernels: none -> 36.4 us  [the longest x4 29.6 us: stage_call(): pl.pallas_call(functools.partial(stage_kernel, count, has_next), out_shap...]
    ppermute x6 -> x30, starting transfers between devices: 29 us -> 53.9 us  [permute(): return lax.ppermute(x, ('grp', 'row'), route)]
    convert_element_type x0 -> x3, other arithmetic: none -> 8.57 us  [the longest x1 6.14 us: sweep(): lower = (precond - upper.astype(F32)).astype(BF16)]
  transfers between devices with their start and end apart: 12 -> 30, of which waited for: 12 -> 12; matrix products, arithmetic and copies ran while one was open for 0% -> 2% of each run, Pallas kernels for 0% -> 10%
where the time goes in v1:
time: 181 us; the launch traced here: 178 us
  waiting for transfers between devices  70.8 us (39%)
  starting transfers between devices  53.9 us (30%)
  Pallas kernels  36.4 us (20%)
  other arithmetic  10.8 us (6%)
  local copies, waits for them, and re-layouts  3.86 us (2%)
    ppermute x30, waiting for transfers between devices, permute(): return lax.ppermute(x, ('grp', 'row'), route)  70.8 us
    ppermute x30, starting transfers between devices, permute(): return lax.ppermute(x, ('grp', 'row'), route)  53.9 us
    pallas_call x4, Pallas kernels, stage_call(): pl.pallas_call(functools.partial(stage_kernel, count, has_next), out_shap...  29.6 us
    pallas_call x2, Pallas kernels, first_call(): pl.pallas_call(functools.partial(first_kernel, count), out_shape=jax.Shap...  6.83 us
    convert_element_type x1, other arithmetic, sweep(): lower = (precond - upper.astype(F32)).astype(BF16)  6.14 us
  transfers between devices with their start and end apart: 30, of which 12 were waited for; matrix products, arithmetic and copies ran while one was open for 2% of the time, Pallas kernels for 10%

profile of v1, /device:TPU:1, one launch (start us, length us, event | category | flops | bytes accessed | tf_op | source)
XLA Modules:
  0.0 178.4 jit_solution(15179294410028038470)
XLA Ops:
  0.6 6.1 %subtract_convert_fusion = (bf16[1024,1024]{1,0:T(8,128)(2,1)S(1)}, bf16[1024,1024]{1,0:T(8,128)(2,1)}) fusion(f32[1024,1024]{1,0:T(8,128)} %param.5), kind=kLoop, calls=%fused_computation | loop fusion | flops 4194304 | bytes 8388608 | tf_op jit(solution)/shard_map/convert_element_type | solution.py:182
  7.3 3.3 %collective-permute-start.3 = (bf16[256,1024]{1,0:T(8,128)(2,1)S(1)}, bf16[256,1024]{1,0:T(8,128)(2,1)S(1)}, u32[]{:S(2)}, u32[]{:S(2)}) collective-permute-start(bf16[256,1024]{1,0:T(8,128)(2,1)S(1)} %copy-done.1), channel_id=1, source_target_pairs={{0,4},{1,5},{2,6},{3,7},{4,0},{5,1},{6,2},{7,3},{8,12},{9,13},{10,... | collective-permute-start | bytes 1572872 | tf_op jit(solution)/shard_map/ppermute | solution.py:166
  10.6 1.0 dynamic-slice_bitcast_fusion.3
  11.6 1.2 collective-permute-start.2
  13.0 24.2 %collective-permute-done.2 = f32[72,256]{1,0:T(8,128)S(1)} collective-permute-done((f32[72,256]{1,0:T(8,128)S(1)}, f32[72,256]{1,0:T(8,128)S(1)}, u32[]{:S(2)}, u32[]{:S(2)}) %collective-permute-start.2) | collective-permute-done | bytes 73760 | tf_op jit(solution)/shard_map/ppermute | solution.py:166
  37.2 0.8 collective-permute-start.4
  38.0 3.3 %collective-permute-done = f32[72,256]{1,0:T(8,128)S(1)} collective-permute-done((f32[72,256]{1,0:T(8,128)S(1)}, f32[72,256]{1,0:T(8,128)S(1)}, u32[]{:S(2)}, u32[]{:S(2)}) %collective-permute-start) | collective-permute-done | bytes 73760 | tf_op jit(solution)/shard_map/ppermute | solution.py:166
  41.3 4.3 %collective-permute-start.6 = (bf16[256,1024]{1,0:T(8,128)(2,1)S(1)}, bf16[256,1024]{1,0:T(8,128)(2,1)S(1)}, u32[]{:S(2)}, u32[]{:S(2)}) collective-permute-start(bf16[256,1024]{1,0:T(8,128)(2,1)S(1)} %copy-done.1), channel_id=1, source_target_pairs={{0,8},{1,9},{2,10},{3,11},{4,12},{5,13},{6,14},{7,15},{8,0},{9,1},... | collective-permute-start | bytes 1572872 | tf_op jit(solution)/shard_map/ppermute | solution.py:166
  45.8 3.3 %collective-permute-done.4.refs_2_ = bf16[256,1024]{1,0:T(8,128)(2,1)} collective-permute-done((bf16[256,1024]{1,0:T(8,128)(2,1)S(1)}, bf16[256,1024]{1,0:T(8,128)(2,1)}, u32[]{:S(2)}, u32[]{:S(2)}) %collective-permute-start.4) | collective-permute-done | bytes 524320 | tf_op jit(solution)/shard_map/ppermute | solution.py:166
  49.1 4.6 %collective-permute-start.7 = (bf16[256,1024]{1,0:T(8,128)(2,1)S(1)}, bf16[256,1024]{1,0:T(8,128)(2,1)}, u32[]{:S(2)}, u32[]{:S(2)}) collective-permute-start(bf16[256,1024]{1,0:T(8,128)(2,1)S(1)} %collective-permute-done.3.refs_1_), channel_id=1, source_target_pairs={{0,8},{1,9},{2,10},{3,11},{4,12},{5,13},{6,14},{7,15},{8,0},{9,1},... | collective-permute-start | bytes 1572872 | tf_op jit(solution)/shard_map/ppermute | solution.py:166
  53.9 6.5 %collective-permute-done.5.refs_3_ = bf16[256,1024]{1,0:T(8,128)(2,1)} collective-permute-done((bf16[256,1024]{1,0:T(8,128)(2,1)S(1)}, bf16[256,1024]{1,0:T(8,128)(2,1)}, u32[]{:S(2)}, u32[]{:S(2)}) %collective-permute-start.5) | collective-permute-done | bytes 524320 | tf_op jit(solution)/shard_map/ppermute | solution.py:166
  60.4 2.5 %collective-permute-start.9 = (bf16[256,1024]{1,0:T(8,128)(2,1)}, bf16[256,1024]{1,0:T(8,128)(2,1)}, u32[]{:S(2)}, u32[]{:S(2)}) collective-permute-start(bf16[256,1024]{1,0:T(8,128)(2,1)} %collective-permute-done.5.refs_3_), channel_id=1, source_target_pairs={{0,8},{1,9},{2,10},{3,11},{4,12},{5,13},{6,14},{7,15},{8,0},{9,1},... | collective-permute-start | bytes 1572872 | tf_op jit(solution)/shard_map/ppermute | solution.py:166
  62.9 0.7 pad_maximum_fusion.r_ref
  63.7 1.1 collective-permute-done.9.refs_7_
  64.8 3.4 %first_corr.2.ca_ref = bf16[72,1024]{1,0:T(8,128)(2,1)} custom-call(s32[1]{0:T(128)} %bitcast.mine_ref, f32[72,1024]{1,0:T(8,128)} %pad_maximum_fusion.r_ref, bf16[256,1024]{1,0:T(8,128)(2,1)} %refs_0_.11, bf16[256,1024]{1,0:T(8,128)(2,1)} %copy-done.3, bf16[256,1024]{1,0:T(8,128)(2,1)} %collective-permute-done.4.refs_2_, ...), custom_call_target="tpu_custom_call" | custom-call | flops 150994944 | bytes 2097152 | tf_op jit(solution)/shard_map/first_corr/pallas_call | solution.py:97
  68.2 4.7 %collective-permute-start.10 = (bf16[72,1024]{1,0:T(8,128)(2,1)}, bf16[72,1024]{1,0:T(8,128)(2,1)S(1)}, u32[]{:S(2)}, u32[]{:S(2)}) collective-permute-start(bf16[72,1024]{1,0:T(8,128)(2,1)} %first_corr.2.ca_ref), channel_id=1, source_target_pairs={{0,2},{1,3},{2,0},{3,1},{4,6},{5,7},{6,4},{7,5},{8,10},{9,11},{10,... | collective-permute-start | bytes 442376 | tf_op jit(solution)/shard_map/ppermute | solution.py:166
  72.9 4.1 %collective-permute-done.10.cb_ref = bf16[72,1024]{1,0:T(8,128)(2,1)S(1)} collective-permute-done((bf16[72,1024]{1,0:T(8,128)(2,1)}, bf16[72,1024]{1,0:T(8,128)(2,1)S(1)}, u32[]{:S(2)}, u32[]{:S(2)}) %collective-permute-start.10) | collective-permute-done | bytes 147488 | tf_op jit(solution)/shard_map/ppermute | solution.py:166
  77.6 7.7 %sweep_stage.4 = (bf16[72,1024]{1,0:T(8,128)(2,1)}, f32[72,1024]{1,0:T(8,128)}, bf16[72,1024]{1,0:T(8,128)(2,1)}, bf16[72,1024]{1,0:T(8,128)(2,1)}) custom-call(s32[1]{0:T(128)} %bitcast.mine_ref, f32[72,1024]{1,0:T(8,128)} %pad_maximum_fusion.r_ref, bf16[72,1024]{1,0:T(8,128)(2,1)} %first_corr.2.ca_ref, bf16[72,1024]{1,0:T(8,128)(2,1)} %copy-done.12, ...), custom_call_target="tpu_custom_call" | custom-call | flops 754974720 | bytes 8388608 | tf_op jit(solution)/shard_map/sweep_stage/pallas_call | solution.py:130
  85.4 1.2 collective-permute-start.13
  86.6 3.0 %collective-permute-done.13.cb_ref = bf16[72,1024]{1,0:T(8,128)(2,1)S(1)} collective-permute-done((bf16[72,1024]{1,0:T(8,128)(2,1)}, bf16[72,1024]{1,0:T(8,128)(2,1)S(1)}, u32[]{:S(2)}, u32[]{:S(2)}) %collective-permute-start.13) | collective-permute-done | bytes 147488 | tf_op jit(solution)/shard_map/ppermute | solution.py:166
  89.6 0.7 copy-done.13
  90.3 7.1 %sweep_stage.5 = (bf16[72,1024]{1,0:T(8,128)(2,1)}, f32[72,1024]{1,0:T(8,128)}, bf16[72,1024]{1,0:T(8,128)(2,1)}) custom-call(s32[1]{0:T(128)S(6)} %sub.37.mine_ref, f32[72,1024]{1,0:T(8,128)} %get-tuple-element.11.r_ref, bf16[72,1024]{1,0:T(8,128)(2,1)} %get-tuple-element.12.ca_ref, bf16[72,1024]{1,0:T(8,128)(2,1)} %copy-done.13, ...), custom_call_target="tpu_custom_call" | custom-call | flops 603979776 | bytes 6291456 | tf_op jit(solution)/shard_map/sweep_stage/pallas_call | solution.py:130
  97.4 3.1 %collective-permute-start.14 = (bf16[72,1024]{1,0:T(8,128)(2,1)}, bf16[72,1024]{1,0:T(8,128)(2,1)S(1)}, u32[]{:S(2)}, u32[]{:S(2)}) collective-permute-start(bf16[72,1024]{1,0:T(8,128)(2,1)} %get-tuple-element.13), channel_id=1, source_target_pairs={{0,16},{1,17},{2,18},{3,19},{4,20},{5,21},{6,22},{7,23},{8,24},{9,... | collective-permute-start | bytes 442376 | tf_op jit(solution)/shard_map/ppermute | solution.py:166
  100.5 2.4 %collective-permute-done.14 = bf16[72,1024]{1,0:T(8,128)(2,1)S(1)} collective-permute-done((bf16[72,1024]{1,0:T(8,128)(2,1)}, bf16[72,1024]{1,0:T(8,128)(2,1)S(1)}, u32[]{:S(2)}, u32[]{:S(2)}) %collective-permute-start.14) | collective-permute-done | bytes 147488 | tf_op jit(solution)/shard_map/ppermute | solution.py:166
  102.9 0.7 convert_element_type.33.r_ref
  103.6 3.4 %first_corr.3.ca_ref = bf16[72,1024]{1,0:T(8,128)(2,1)} custom-call(s32[1]{0:T(128)} %bitcast.mine_ref, f32[72,1024]{1,0:T(8,128)} %convert_element_type.33.r_ref, bf16[256,1024]{1,0:T(8,128)(2,1)} %refs_0_.11, bf16[256,1024]{1,0:T(8,128)(2,1)} %copy-done.3, bf16[256,1024]{1,0:T(8,128)(2,1)} %collective-permute-done.4.refs_2_, ...), custom_call_target="tpu_custom_call" | custom-call | flops 150994944 | bytes 2097152 | tf_op jit(solution)/shard_map/first_corr/pallas_call | solution.py:97
  107.1 1.2 collective-permute-start.15
  108.4 3.7 %collective-permute-start.25 = (bf16[72,1024]{1,0:T(8,128)(2,1)S(1)}, bf16[72,1024]{1,0:T(8,128)(2,1)S(1)}, u32[]{:S(2)}, u32[]{:S(2)}) collective-permute-start(bf16[72,1024]{1,0:T(8,128)(2,1)S(1)} %collective-permute-done.14), channel_id=1, source_target_pairs={{0,8},{1,9},{2,10},{3,11},{4,12},{5,13},{6,14},{7,15},{8,0},{9,1},... | collective-permute-start | bytes 442376 | tf_op jit(solution)/shard_map/ppermute | solution.py:166
  112.1 0.7 copy-done.10
  112.8 7.7 %sweep_stage.6 = (bf16[72,1024]{1,0:T(8,128)(2,1)}, f32[72,1024]{1,0:T(8,128)}, bf16[72,1024]{1,0:T(8,128)(2,1)}, bf16[72,1024]{1,0:T(8,128)(2,1)}) custom-call(s32[1]{0:T(128)} %bitcast.mine_ref, f32[72,1024]{1,0:T(8,128)} %convert_element_type.33.r_ref, bf16[72,1024]{1,0:T(8,128)(2,1)} %first_corr.3.ca_ref, bf16[72,1024]{1,0:T(8,128)(2,1)} %copy-done.10, ...), custom_call_target="tpu_custom_call" | custom-call | flops 754974720 | bytes 8388608 | tf_op jit(solution)/shard_map/sweep_stage/pallas_call | solution.py:130
  121.0 7.1 %collective-permute-start.16 = (bf16[72,1024]{1,0:T(8,128)(2,1)S(1)}, bf16[72,1024]{1,0:T(8,128)(2,1)S(1)}, u32[]{:S(2)}, u32[]{:S(2)}) collective-permute-start(bf16[72,1024]{1,0:T(8,128)(2,1)S(1)} %broadcast_select_fusion.1), channel_id=1, source_target_pairs={{8,0},{9,1},{10,2},{11,3},{12,4},{13,5},{14,6},{15,7},{24,16},{25,... | collective-permute-start | bytes 442376 | tf_op jit(solution)/shard_map/ppermute | solution.py:166
  128.6 3.2 %collective-permute-start.28 = (bf16[144,256]{1,0:T(8,128)(2,1)S(1)}, bf16[144,256]{1,0:T(8,128)(2,1)S(1)}, u32[]{:S(2)}, u32[]{:S(2)}) collective-permute-start(bf16[144,256]{1,0:T(8,128)(2,1)S(1)} %get-tuple-element.26), channel_id=1, source_target_pairs={{0,5},{1,4},{2,7},{3,6},{4,1},{5,0},{6,3},{7,2},{8,13},{9,12},{10,... | collective-permute-start | bytes 221192 | tf_op jit(solution)/shard_map/ppermute | solution.py:166
  132.5 7.1 %sweep_stage.7 = (bf16[72,1024]{1,0:T(8,128)(2,1)}, f32[72,1024]{1,0:T(8,128)}, bf16[72,1024]{1,0:T(8,128)(2,1)}) custom-call(s32[1]{0:T(128)S(6)} %sub.37.mine_ref, f32[72,1024]{1,0:T(8,128)} %get-tuple-element.16.r_ref, bf16[72,1024]{1,0:T(8,128)(2,1)} %get-tuple-element.17.ca_ref, bf16[72,1024]{1,0:T(8,128)(2,1)} %copy-done.11, ...), custom_call_target="tpu_custom_call" | custom-call | flops 603979776 | bytes 6291456 | tf_op jit(solution)/shard_map/sweep_stage/pallas_call | solution.py:130
  139.7 1.3 collective-permute-start.18
  141.0 1.9 %collective-permute-done.18 = bf16[72,1024]{1,0:T(8,128)(2,1)S(1)} collective-permute-done((bf16[72,1024]{1,0:T(8,128)(2,1)S(1)}, bf16[72,1024]{1,0:T(8,128)(2,1)S(1)}, u32[]{:S(2)}, u32[]{:S(2)}) %collective-permute-start.18) | collective-permute-done | bytes 147488 | tf_op jit(solution)/shard_map/ppermute | solution.py:166
  143.2 0.7 collective-permute-start.19
  143.9 2.0 %collective-permute-start.20 = (bf16[144,1024]{1,0:T(8,128)(2,1)S(1)}, bf16[144,1024]{1,0:T(8,128)(2,1)S(1)}, u32[]{:S(2)}, u32[]{:S(2)}) collective-permute-start(bf16[144,1024]{1,0:T(8,128)(2,1)S(1)} %get-tuple-element.29), channel_id=1, source_target_pairs={{8,12},{9,13},{10,14},{11,15},{12,8},{13,9},{14,10},{15,11},{24,28... | collective-permute-start | bytes 884744 | tf_op jit(solution)/shard_map/ppermute | solution.py:166
  145.9 0.7 collective-permute-start.21
  146.6 2.1 %collective-permute-start.22 = (bf16[144,1024]{1,0:T(8,128)(2,1)S(1)}, bf16[144,1024]{1,0:T(8,128)(2,1)S(1)}, u32[]{:S(2)}, u32[]{:S(2)}) collective-permute-start(bf16[144,1024]{1,0:T(8,128)(2,1)S(1)} %get-tuple-element.29), channel_id=1, source_target_pairs={{8,9},{9,8},{10,11},{11,10},{12,13},{13,12},{14,15},{15,14},{24,25... | collective-permute-start | bytes 884744 | tf_op jit(solution)/shard_map/ppermute | solution.py:166
  148.8 0.7 collective-permute-start.23
  149.5 12.2 %collective-permute-done.20 = bf16[144,1024]{1,0:T(8,128)(2,1)S(1)} collective-permute-done((bf16[144,1024]{1,0:T(8,128)(2,1)S(1)}, bf16[144,1024]{1,0:T(8,128)(2,1)S(1)}, u32[]{:S(2)}, u32[]{:S(2)}) %collective-permute-start.20) | collective-permute-done | bytes 294944 | tf_op jit(solution)/shard_map/ppermute | solution.py:166
  161.7 2.1 %collective-permute-start.24 = (bf16[144,1024]{1,0:T(8,128)(2,1)S(1)}, bf16[144,1024]{1,0:T(8,128)(2,1)S(1)}, u32[]{:S(2)}, u32[]{:S(2)}) collective-permute-start(bf16[144,1024]{1,0:T(8,128)(2,1)S(1)} %collective-permute-done.20), channel_id=1, source_target_pairs={{8,9},{9,8},{10,11},{11,10},{12,13},{13,12},{14,15},{15,14},{24,25... | collective-permute-start | bytes 884744 | tf_op jit(solution)/shard_map/ppermute | solution.py:166
  164.0 7.7 %collective-permute-done.24 = bf16[144,1024]{1,0:T(8,128)(2,1)S(1)} collective-permute-done((bf16[144,1024]{1,0:T(8,128)(2,1)S(1)}, bf16[144,1024]{1,0:T(8,128)(2,1)S(1)}, u32[]{:S(2)}, u32[]{:S(2)}) %collective-permute-start.24) | collective-permute-done | bytes 294944 | tf_op jit(solution)/shard_map/ppermute | solution.py:166
  171.8 1.6 fusion.5
  173.4 1.3 collective-permute-start.29
  174.7 1.7 convert_bitcast_fusion
  176.4 1.0 collective-permute-done.29
  177.4 0.9 select_bitcast_fusion
  (67 shorter events, 4.0 us)
Async XLA Ops:
  0.6 6.7 %copy-start.1 = (bf16[256,1024]{1,0:T(8,128)(2,1)S(1)}, bf16[256,1024]{1,0:T(8,128)(2,1)}, u32[]{:S(2)}) copy-start(bf16[256,1024]{1,0:T(8,128)(2,1)} %refs_0_.11) | copy-start | bytes 1572868
  6.8 61.4 %copy-start = (bf16[1024,1024]{1,0:T(8,128)(2,1)}, bf16[1024,1024]{1,0:T(8,128)(2,1)S(1)}, u32[]{:S(2)}) copy-start(bf16[1024,1024]{1,0:T(8,128)(2,1)S(1)} %get-tuple-element.20.refs_10_) | copy-start | bytes 6291460
  6.8 70.2 %collective-permute-start.11 = (bf16[1024,1024]{1,0:T(8,128)(2,1)}, bf16[1024,1024]{1,0:T(8,128)(2,1)}, u32[]{:S(2)}, u32[]{:S(2)}) collective-permute-start(bf16[1024,1024]{1,0:T(8,128)(2,1)} %get-tuple-element.21.refs_8_), channel_id=1, source_target_pairs={{0,8},{1,9},{2,10},{3,11},{4,12},{5,13},{6,14},{7,15},{8,0},{9,1},... | collective-permute-start | bytes 6291464 | tf_op jit(solution)/shard_map/ppermute | solution.py:166
  6.8 70.2 %collective-permute-start.12 = (bf16[1024,1024]{1,0:T(8,128)(2,1)S(1)}, bf16[1024,1024]{1,0:T(8,128)(2,1)}, u32[]{:S(2)}, u32[]{:S(2)}) collective-permute-start(bf16[1024,1024]{1,0:T(8,128)(2,1)S(1)} %get-tuple-element.20.refs_10_), channel_id=1, source_target_pairs={{0,8},{1,9},{2,10},{3,11},{4,12},{5,13},{6,14},{7,15},{8,0},{9,1},... | collective-permute-start | bytes 6291464 | tf_op jit(solution)/shard_map/ppermute | solution.py:166
  7.3 38.3 %collective-permute-start.3 = (bf16[256,1024]{1,0:T(8,128)(2,1)S(1)}, bf16[256,1024]{1,0:T(8,128)(2,1)S(1)}, u32[]{:S(2)}, u32[]{:S(2)}) collective-permute-start(bf16[256,1024]{1,0:T(8,128)(2,1)S(1)} %copy-done.1), channel_id=1, source_target_pairs={{0,4},{1,5},{2,6},{3,7},{4,0},{5,1},{6,2},{7,3},{8,12},{9,13},{10,... | collective-permute-start | bytes 1572872 | tf_op jit(solution)/shard_map/ppermute | solution.py:166
  11.6 25.6 %collective-permute-start.2 = (f32[72,256]{1,0:T(8,128)S(1)}, f32[72,256]{1,0:T(8,128)S(1)}, u32[]{:S(2)}, u32[]{:S(2)}) collective-permute-start(f32[72,256]{1,0:T(8,128)S(1)} %get-tuple-element.23), channel_id=1, source_target_pairs={{0,5},{1,4},{2,7},{3,6},{4,1},{5,0},{6,3},{7,2},{8,13},{9,12},{10,... | collective-permute-start | bytes 221192 | tf_op jit(solution)/shard_map/ppermute | solution.py:166
  12.8 24.4 %collective-permute-start.1 = (f32[72,256]{1,0:T(8,128)S(1)}, f32[72,256]{1,0:T(8,128)S(1)}, u32[]{:S(2)}, u32[]{:S(2)}) collective-permute-start(f32[72,256]{1,0:T(8,128)S(1)} %get-tuple-element.24), channel_id=1, source_target_pairs={{0,1},{1,0},{2,3},{3,2},{4,5},{5,4},{6,7},{7,6},{8,9},{9,8},{10,11... | collective-permute-start | bytes 221192 | tf_op jit(solution)/shard_map/ppermute | solution.py:166
  37.2 4.1 %collective-permute-start = (f32[72,256]{1,0:T(8,128)S(1)}, f32[72,256]{1,0:T(8,128)S(1)}, u32[]{:S(2)}, u32[]{:S(2)}) collective-permute-start(f32[72,256]{1,0:T(8,128)S(1)} %get-tuple-element.25), channel_id=1, source_target_pairs={{0,4},{1,5},{2,6},{3,7},{4,0},{5,1},{6,2},{7,3},{8,12},{9,13},{10,... | collective-permute-start | bytes 221192 | tf_op jit(solution)/shard_map/ppermute | solution.py:166
  37.2 11.9 %collective-permute-start.4 = (bf16[256,1024]{1,0:T(8,128)(2,1)S(1)}, bf16[256,1024]{1,0:T(8,128)(2,1)}, u32[]{:S(2)}, u32[]{:S(2)}) collective-permute-start(bf16[256,1024]{1,0:T(8,128)(2,1)S(1)} %copy-done.1), channel_id=1, source_target_pairs={{0,1},{1,0},{2,3},{3,2},{4,5},{5,4},{6,7},{7,6},{8,9},{9,8},{10,11... | collective-permute-start | bytes 1572872 | tf_op jit(solution)/shard_map/ppermute | solution.py:166
  41.3 12.5 %collective-permute-start.6 = (bf16[256,1024]{1,0:T(8,128)(2,1)S(1)}, bf16[256,1024]{1,0:T(8,128)(2,1)S(1)}, u32[]{:S(2)}, u32[]{:S(2)}) collective-permute-start(bf16[256,1024]{1,0:T(8,128)(2,1)S(1)} %copy-done.1), channel_id=1, source_target_pairs={{0,8},{1,9},{2,10},{3,11},{4,12},{5,13},{6,14},{7,15},{8,0},{9,1},... | collective-permute-start | bytes 1572872 | tf_op jit(solution)/shard_map/ppermute | solution.py:166
  45.6 19.2 %copy-start.3 = (bf16[256,1024]{1,0:T(8,128)(2,1)}, bf16[256,1024]{1,0:T(8,128)(2,1)S(1)}, u32[]{:S(2)}) copy-start(bf16[256,1024]{1,0:T(8,128)(2,1)S(1)} %collective-permute-done.3.refs_1_) | copy-start | bytes 1572868
  45.6 14.8 %collective-permute-start.5 = (bf16[256,1024]{1,0:T(8,128)(2,1)S(1)}, bf16[256,1024]{1,0:T(8,128)(2,1)}, u32[]{:S(2)}, u32[]{:S(2)}) collective-permute-start(bf16[256,1024]{1,0:T(8,128)(2,1)S(1)} %collective-permute-done.3.refs_1_), channel_id=1, source_target_pairs={{0,1},{1,0},{2,3},{3,2},{4,5},{5,4},{6,7},{7,6},{8,9},{9,8},{10,11... | collective-permute-start | bytes 1572872 | tf_op jit(solution)/shard_map/ppermute | solution.py:166
  49.1 14.5 %collective-permute-start.7 = (bf16[256,1024]{1,0:T(8,128)(2,1)S(1)}, bf16[256,1024]{1,0:T(8,128)(2,1)}, u32[]{:S(2)}, u32[]{:S(2)}) collective-permute-start(bf16[256,1024]{1,0:T(8,128)(2,1)S(1)} %collective-permute-done.3.refs_1_), channel_id=1, source_target_pairs={{0,8},{1,9},{2,10},{3,11},{4,12},{5,13},{6,14},{7,15},{8,0},{9,1},... | collective-permute-start | bytes 1572872 | tf_op jit(solution)/shard_map/ppermute | solution.py:166
  53.8 6.6 %copy-start.4 = (bf16[256,1024]{1,0:T(8,128)(2,1)}, bf16[256,1024]{1,0:T(8,128)(2,1)S(1)}, u32[]{:S(2)}) copy-start(bf16[256,1024]{1,0:T(8,128)(2,1)S(1)} %collective-permute-done.6.refs_4_) | copy-start | bytes 1572868
  53.8 9.9 %collective-permute-start.8 = (bf16[256,1024]{1,0:T(8,128)(2,1)}, bf16[256,1024]{1,0:T(8,128)(2,1)S(1)}, u32[]{:S(2)}, u32[]{:S(2)}) collective-permute-start(bf16[256,1024]{1,0:T(8,128)(2,1)} %collective-permute-done.4.refs_2_), channel_id=1, source_target_pairs={{0,8},{1,9},{2,10},{3,11},{4,12},{5,13},{6,14},{7,15},{8,0},{9,1},... | collective-permute-start | bytes 1572872 | tf_op jit(solution)/shard_map/ppermute | solution.py:166
  60.4 4.4 %collective-permute-start.9 = (bf16[256,1024]{1,0:T(8,128)(2,1)}, bf16[256,1024]{1,0:T(8,128)(2,1)}, u32[]{:S(2)}, u32[]{:S(2)}) collective-permute-start(bf16[256,1024]{1,0:T(8,128)(2,1)} %collective-permute-done.5.refs_3_), channel_id=1, source_target_pairs={{0,8},{1,9},{2,10},{3,11},{4,12},{5,13},{6,14},{7,15},{8,0},{9,1},... | collective-permute-start | bytes 1572872 | tf_op jit(solution)/shard_map/ppermute | solution.py:166
  63.7 1.1 copy-start.5
  68.2 8.8 %collective-permute-start.10 = (bf16[72,1024]{1,0:T(8,128)(2,1)}, bf16[72,1024]{1,0:T(8,128)(2,1)S(1)}, u32[]{:S(2)}, u32[]{:S(2)}) collective-permute-start(bf16[72,1024]{1,0:T(8,128)(2,1)} %first_corr.2.ca_ref), channel_id=1, source_target_pairs={{0,2},{1,3},{2,0},{3,1},{4,6},{5,7},{6,4},{7,5},{8,10},{9,11},{10,... | collective-permute-start | bytes 442376 | tf_op jit(solution)/shard_map/ppermute | solution.py:166
  77.0 0.7 copy-start.12
  85.4 4.3 %collective-permute-start.13 = (bf16[72,1024]{1,0:T(8,128)(2,1)}, bf16[72,1024]{1,0:T(8,128)(2,1)S(1)}, u32[]{:S(2)}, u32[]{:S(2)}) collective-permute-start(bf16[72,1024]{1,0:T(8,128)(2,1)} %get-tuple-element.12.ca_ref), channel_id=1, source_target_pairs={{0,2},{1,3},{2,0},{3,1},{4,6},{5,7},{6,4},{7,5},{8,10},{9,11},{10,... | collective-permute-start | bytes 442376 | tf_op jit(solution)/shard_map/ppermute | solution.py:166
  89.6 0.7 copy-start.13
  97.4 5.5 %collective-permute-start.14 = (bf16[72,1024]{1,0:T(8,128)(2,1)}, bf16[72,1024]{1,0:T(8,128)(2,1)S(1)}, u32[]{:S(2)}, u32[]{:S(2)}) collective-permute-start(bf16[72,1024]{1,0:T(8,128)(2,1)} %get-tuple-element.13), channel_id=1, source_target_pairs={{0,16},{1,17},{2,18},{3,19},{4,20},{5,21},{6,22},{7,23},{8,24},{9,... | collective-permute-start | bytes 442376 | tf_op jit(solution)/shard_map/ppermute | solution.py:166
  103.6 4.7 %copy-start.6 = (f32[256,576]{0,1:T(8,128)S(1)}, f32[256,576]{0,1:T(8,128)}, u32[]{:S(2)}) copy-start(f32[256,576]{0,1:T(8,128)} %param.4) | copy-start | bytes 1769476
  107.1 5.1 %collective-permute-start.15 = (bf16[72,1024]{1,0:T(8,128)(2,1)}, bf16[72,1024]{1,0:T(8,128)(2,1)S(1)}, u32[]{:S(2)}, u32[]{:S(2)}) collective-permute-start(bf16[72,1024]{1,0:T(8,128)(2,1)} %first_corr.3.ca_ref), channel_id=1, source_target_pairs={{0,2},{1,3},{2,0},{3,1},{4,6},{5,7},{6,4},{7,5},{8,10},{9,11},{10,... | collective-permute-start | bytes 442376 | tf_op jit(solution)/shard_map/ppermute | solution.py:166
  108.4 12.6 %copy-start.9 = (bf16[72,1024]{1,0:T(8,128)(2,1)S(1)}, bf16[72,1024]{1,0:T(8,128)(2,1)}, u32[]{:S(2)}) copy-start(bf16[72,1024]{1,0:T(8,128)(2,1)} %get-tuple-element.15) | copy-start | bytes 442372
  108.4 19.7 %collective-permute-start.25 = (bf16[72,1024]{1,0:T(8,128)(2,1)S(1)}, bf16[72,1024]{1,0:T(8,128)(2,1)S(1)}, u32[]{:S(2)}, u32[]{:S(2)}) collective-permute-start(bf16[72,1024]{1,0:T(8,128)(2,1)S(1)} %collective-permute-done.14), channel_id=1, source_target_pairs={{0,8},{1,9},{2,10},{3,11},{4,12},{5,13},{6,14},{7,15},{8,0},{9,1},... | collective-permute-start | bytes 442376 | tf_op jit(solution)/shard_map/ppermute | solution.py:166
  112.1 0.7 copy-start.10
  120.5 11.4 %collective-permute-start.17 = (bf16[72,1024]{1,0:T(8,128)(2,1)}, bf16[72,1024]{1,0:T(8,128)(2,1)S(1)}, u32[]{:S(2)}, u32[]{:S(2)}) collective-permute-start(bf16[72,1024]{1,0:T(8,128)(2,1)} %get-tuple-element.17.ca_ref), channel_id=1, source_target_pairs={{0,2},{1,3},{2,0},{3,1},{4,6},{5,7},{6,4},{7,5},{8,10},{9,11},{10,... | collective-permute-start | bytes 442376 | tf_op jit(solution)/shard_map/ppermute | solution.py:166
  121.0 20.0 %collective-permute-start.16 = (bf16[72,1024]{1,0:T(8,128)(2,1)S(1)}, bf16[72,1024]{1,0:T(8,128)(2,1)S(1)}, u32[]{:S(2)}, u32[]{:S(2)}) collective-permute-start(bf16[72,1024]{1,0:T(8,128)(2,1)S(1)} %broadcast_select_fusion.1), channel_id=1, source_target_pairs={{8,0},{9,1},{10,2},{11,3},{12,4},{13,5},{14,6},{15,7},{24,16},{25,... | collective-permute-start | bytes 442376 | tf_op jit(solution)/shard_map/ppermute | solution.py:166
  128.2 12.7 %collective-permute-start.26 = (bf16[144,256]{1,0:T(8,128)(2,1)S(1)}, bf16[144,256]{1,0:T(8,128)(2,1)S(1)}, u32[]{:S(2)}, u32[]{:S(2)}) collective-permute-start(bf16[144,256]{1,0:T(8,128)(2,1)S(1)} %get-tuple-element.28), channel_id=1, source_target_pairs={{0,4},{1,5},{2,6},{3,7},{4,0},{5,1},{6,2},{7,3},{8,12},{9,13},{10,... | collective-permute-start | bytes 221192 | tf_op jit(solution)/shard_map/ppermute | solution.py:166
  128.3 17.6 %collective-permute-start.27 = (bf16[144,256]{1,0:T(8,128)(2,1)S(1)}, bf16[144,256]{1,0:T(8,128)(2,1)S(1)}, u32[]{:S(2)}, u32[]{:S(2)}) collective-permute-start(bf16[144,256]{1,0:T(8,128)(2,1)S(1)} %get-tuple-element.27), channel_id=1, source_target_pairs={{0,1},{1,0},{2,3},{3,2},{4,5},{5,4},{6,7},{7,6},{8,9},{9,8},{10,11... | collective-permute-start | bytes 221192 | tf_op jit(solution)/shard_map/ppermute | solution.py:166
  128.6 20.2 %collective-permute-start.28 = (bf16[144,256]{1,0:T(8,128)(2,1)S(1)}, bf16[144,256]{1,0:T(8,128)(2,1)S(1)}, u32[]{:S(2)}, u32[]{:S(2)}) collective-permute-start(bf16[144,256]{1,0:T(8,128)(2,1)S(1)} %get-tuple-element.26), channel_id=1, source_target_pairs={{0,5},{1,4},{2,7},{3,6},{4,1},{5,0},{6,3},{7,2},{8,13},{9,12},{10,... | collective-permute-start | bytes 221192 | tf_op jit(solution)/shard_map/ppermute | solution.py:166
  131.9 0.7 copy-start.11
  132.5 7.1 %copy-start.8 = (bf16[72,1024]{1,0:T(8,128)(2,1)S(1)}, bf16[72,1024]{1,0:T(8,128)(2,1)}, u32[]{:S(2)}) copy-start(bf16[72,1024]{1,0:T(8,128)(2,1)} %get-tuple-element.19) | copy-start | bytes 442372
  139.7 3.3 %collective-permute-start.18 = (bf16[72,1024]{1,0:T(8,128)(2,1)S(1)}, bf16[72,1024]{1,0:T(8,128)(2,1)S(1)}, u32[]{:S(2)}, u32[]{:S(2)}) collective-permute-start(bf16[72,1024]{1,0:T(8,128)(2,1)S(1)} %broadcast_select_fusion), channel_id=1, source_target_pairs={{0,8},{1,9},{2,10},{3,11},{4,12},{5,13},{6,14},{7,15},{16,24},{17,... | collective-permute-start | bytes 442376 | tf_op jit(solution)/shard_map/ppermute | solution.py:166
  143.2 5.6 %collective-permute-start.19 = (bf16[144,1024]{1,0:T(8,128)(2,1)S(1)}, bf16[144,1024]{1,0:T(8,128)(2,1)S(1)}, u32[]{:S(2)}, u32[]{:S(2)}) collective-permute-start(bf16[144,1024]{1,0:T(8,128)(2,1)S(1)} %get-tuple-element.31), channel_id=1, source_target_pairs={{0,4},{1,5},{2,6},{3,7},{4,0},{5,1},{6,2},{7,3},{16,20},{17,21},{1... | collective-permute-start | bytes 884744 | tf_op jit(solution)/shard_map/ppermute | solution.py:166
  143.9 17.8 %collective-permute-start.20 = (bf16[144,1024]{1,0:T(8,128)(2,1)S(1)}, bf16[144,1024]{1,0:T(8,128)(2,1)S(1)}, u32[]{:S(2)}, u32[]{:S(2)}) collective-permute-start(bf16[144,1024]{1,0:T(8,128)(2,1)S(1)} %get-tuple-element.29), channel_id=1, source_target_pairs={{8,12},{9,13},{10,14},{11,15},{12,8},{13,9},{14,10},{15,11},{24,28... | collective-permute-start | bytes 884744 | tf_op jit(solution)/shard_map/ppermute | solution.py:166
  145.9 18.0 %collective-permute-start.21 = (bf16[144,1024]{1,0:T(8,128)(2,1)S(1)}, bf16[144,1024]{1,0:T(8,128)(2,1)S(1)}, u32[]{:S(2)}, u32[]{:S(2)}) collective-permute-start(bf16[144,1024]{1,0:T(8,128)(2,1)S(1)} %get-tuple-element.31), channel_id=1, source_target_pairs={{0,1},{1,0},{2,3},{3,2},{4,5},{5,4},{6,7},{7,6},{16,17},{17,16},{1... | collective-permute-start | bytes 884744 | tf_op jit(solution)/shard_map/ppermute | solution.py:166
  146.6 17.3 %collective-permute-start.22 = (bf16[144,1024]{1,0:T(8,128)(2,1)S(1)}, bf16[144,1024]{1,0:T(8,128)(2,1)S(1)}, u32[]{:S(2)}, u32[]{:S(2)}) collective-permute-start(bf16[144,1024]{1,0:T(8,128)(2,1)S(1)} %get-tuple-element.29), channel_id=1, source_target_pairs={{8,9},{9,8},{10,11},{11,10},{12,13},{13,12},{14,15},{15,14},{24,25... | collective-permute-start | bytes 884744 | tf_op jit(solution)/shard_map/ppermute | solution.py:166
  148.8 22.9 %copy-start.7 = (f32[576,256]{1,0:T(8,128)}, f32[576,256]{1,0:T(8,128)S(1)}, u32[]{:S(2)}) copy-start(f32[576,256]{1,0:T(8,128)S(1)} %fusion) | copy-start | bytes 1769476
  148.8 15.2 %collective-permute-start.23 = (bf16[144,1024]{1,0:T(8,128)(2,1)S(1)}, bf16[144,1024]{1,0:T(8,128)(2,1)S(1)}, u32[]{:S(2)}, u32[]{:S(2)}) collective-permute-start(bf16[144,1024]{1,0:T(8,128)(2,1)S(1)} %collective-permute-done.19), channel_id=1, source_target_pairs={{0,1},{1,0},{2,3},{3,2},{4,5},{5,4},{6,7},{7,6},{16,17},{17,16},{1... | collective-permute-start | bytes 884744 | tf_op jit(solution)/shard_map/ppermute | solution.py:166
  161.7 10.1 %collective-permute-start.24 = (bf16[144,1024]{1,0:T(8,128)(2,1)S(1)}, bf16[144,1024]{1,0:T(8,128)(2,1)S(1)}, u32[]{:S(2)}, u32[]{:S(2)}) collective-permute-start(bf16[144,1024]{1,0:T(8,128)(2,1)S(1)} %collective-permute-done.20), channel_id=1, source_target_pairs={{8,9},{9,8},{10,11},{11,10},{12,13},{13,12},{14,15},{15,14},{24,25... | collective-permute-start | bytes 884744 | tf_op jit(solution)/shard_map/ppermute | solution.py:166
  163.8 8.0 %copy-start.2 = (bf16[256,1024]{1,0:T(8,128)(2,1)S(1)}, bf16[256,1024]{1,0:T(8,128)(2,1)}, u32[]{:S(2)}) copy-start(bf16[256,1024]{1,0:T(8,128)(2,1)} %refs_0_.11) | copy-start | bytes 1572868
  173.4 4.0 %collective-permute-start.29 = (f32[576,256]{1,0:T(8,128)S(1)}, f32[576,256]{1,0:T(8,128)S(1)}, u32[]{:S(2)}, u32[]{:S(2)}) collective-permute-start(f32[576,256]{1,0:T(8,128)S(1)} %get-tuple-element.32), channel_id=1, source_target_pairs={{0,8},{1,9},{2,10},{3,11},{4,12},{5,13},{6,14},{7,15},{16,24},{17,... | collective-permute-start | bytes 1769480 | tf_op jit(solution)/shard_map/ppermute | solution.py:166
